TPU v7x, 32 devices: a whole 2x2x4 slice. The times are simulated.
32 devices in a mesh: fsdp: 2 (over x), ctx: 4 (over y, core), tp: 4 (over z).
Axes of the slice: x: 2, y: 2, z: 4, core: 2. Of those that a mesh axis runs over, the one named last changes fastest.
Arguments:
- inputs: bfloat16 [8, 2048, 768], P('fsdp', ('ctx', 'tp')), may hold values from -6 to 6
- segments: int32 [8, 2048], P('fsdp'), may hold values from 0 to 15, never falling along the last dimension, each value on 1 to 1024 neighbouring positions
- query_weight: bfloat16 [768, 768], P(('fsdp', 'ctx'), 'tp'), may hold values from -0.3125 to 0.3125
- query_bias: float32 [768], P('tp'), may hold values from -1.5 to 1.5
- key_weight: bfloat16 [768, 768], P(('fsdp', 'ctx'), 'tp'), may hold values from -0.3125 to 0.3125
- value_weight: bfloat16 [768, 768], P(('fsdp', 'ctx'), 'tp'), may hold values from -0.21875 to 0.21875
- value_bias: float32 [768], P('tp'), may hold values from -1.5 to 1.5
- output_weight: bfloat16 [768, 768], P('tp', ('fsdp', 'ctx')), may hold values from -1.25 to 1.25
- output_bias: float32 [768], replicated, may hold values from -1.5 to 1.5
- first_gain: float32 [768], replicated, may hold values from 0.5 to 1.5
- first_shift: float32 [768], replicated, may hold values from -1.5 to 1.5
- expand_weight: bfloat16 [768, 3072], P(('fsdp', 'ctx'), 'tp'), may hold values from -0.21875 to 0.21875
- expand_bias: float32 [3072], P('tp'), may hold values from -1.5 to 1.5
- contract_weight: bfloat16 [3072, 768], P('tp', ('fsdp', 'ctx')), may hold values from -0.15625 to 0.15625
- contract_bias: float32 [768], replicated, may hold values from -1.5 to 1.5
- second_gain: float32 [768], replicated, may hold values from 0.5 to 1.5
- second_shift: float32 [768], replicated, may hold values from -1.5 to 1.5
- cotangent: bfloat16 [8, 2048, 768], P('fsdp', ('ctx', 'tp')), may hold values from -6 to 6
Outputs:
- outputs: bfloat16 [8, 2048, 768], P('fsdp', ('ctx', 'tp'))
- input_grad: bfloat16 [8, 2048, 768], P('fsdp', ('ctx', 'tp'))
- query_weight_grad: float32 [768, 768], P(('fsdp', 'ctx'), 'tp')
- query_bias_grad: float32 [768], P('tp')
- key_weight_grad: float32 [768, 768], P(('fsdp', 'ctx'), 'tp')
- value_weight_grad: float32 [768, 768], P(('fsdp', 'ctx'), 'tp')
- value_bias_grad: float32 [768], P('tp')
- output_weight_grad: float32 [768, 768], P('tp', ('fsdp', 'ctx'))
- output_bias_grad: float32 [768], replicated
- first_gain_grad: float32 [768], replicated
- first_shift_grad: float32 [768], replicated
- expand_weight_grad: float32 [768, 3072], P(('fsdp', 'ctx'), 'tp')
- expand_bias_grad: float32 [3072], P('tp')
- contract_weight_grad: float32 [3072, 768], P('tp', ('fsdp', 'ctx'))
- contract_bias_grad: float32 [768], replicated
- second_gain_grad: float32 [768], replicated
- second_shift_grad: float32 [768], replicated
Inputs may be any that keep to these rules, and one draw needn't show every extreme that they name: `segments`: along each sequence the segment numbers never fall and take every value 0 to 15; a document has at most 1024 tokens, and one document of each sequence has exactly 1024.
All inputs are finite; a program needn't handle non-finite values.
Results may differ from a plain program's by a relative error of at most 0.022.
Values may be sent and summed in bfloat16 or wider, within the bound.
No kernel may reach another device: no remote copies, remote signals or barrier semaphores. Data moves between devices by JAX's collectives and lax.ppermute only.
A program may use at most 192 MiB of HBM per device.

v0:
```python
import jax
import jax.numpy as jnp
from jax import lax
from jax.sharding import PartitionSpec as P

HEAD_DIM = 64
epsilon = 1e-05
masked_value = -1e30


def in_blocks(value, dim, count):
    lengths = value.shape
    tiles = value.reshape(*lengths[:dim], count, lengths[dim] // count, *lengths[dim + 1 :])
    return jnp.moveaxis(tiles, dim, 0)


def sent_and_summed(value, axis, dim):
    count = lax.axis_size(axis)
    tiles = lax.all_to_all(in_blocks(value, dim, count), axis, 0, 0, tiled=True)
    return jnp.sum(tiles.astype(jnp.float32), axis=0)


def in_one_piece(arrays, axis, dim, along):
    both = jnp.concatenate(arrays, axis=along)
    out, at, done = (sent_and_summed(both, axis, dim), 0, [])
    for a in arrays:
        done.append(lax.slice_in_dim(out, at, at + a.shape[along], axis=along))
        at += a.shape[along]
    return tuple(done)


def exact_gelu(values):
    return jax.nn.gelu(values, approximate=False)


def whole_rows(tensor):
    return lax.all_gather(tensor, "tp", axis=1, tiled=True)


def feature_sum(tensor):
    return lax.psum_scatter(
        tensor.astype(jnp.bfloat16), "tp", scatter_dimension=1, tiled=True
    ).astype(jnp.float32)


def fetch_weights(
    query_weight, key_weight, value_weight, expand_weight, output_weight, contract_weight
):
    front_set = (
        lax.all_gather(query_weight, ("fsdp", "ctx"), axis=0, tiled=True),
        lax.all_gather(key_weight, ("fsdp", "ctx"), axis=0, tiled=True),
        lax.all_gather(value_weight, ("fsdp", "ctx"), axis=0, tiled=True),
        lax.all_gather(expand_weight, ("fsdp", "ctx"), axis=0, tiled=True),
    )
    back_set = (
        lax.all_gather(output_weight, ("fsdp", "ctx"), axis=1, tiled=True),
        lax.all_gather(contract_weight, ("fsdp", "ctx"), axis=1, tiled=True),
    )
    return (front_set, back_set)


def fetch_blocks(keys_low, values_low):
    return (
        lax.all_gather(keys_low, "ctx", axis=1, tiled=True),
        lax.all_gather(values_low, "ctx", axis=1, tiled=True),
    )


def to_items(tensor):
    seq_count, row_count, feat_count = tensor.shape
    heads_here = feat_count // HEAD_DIM
    shaped = tensor.reshape(seq_count, row_count, heads_here, HEAD_DIM).transpose(0, 2, 1, 3)
    return shaped.reshape(seq_count * heads_here, row_count, HEAD_DIM)


def from_items(tensor, seq_count):
    item_count, row_count, _ = tensor.shape
    heads_here = item_count // seq_count
    shaped = tensor.reshape(seq_count, heads_here, row_count, HEAD_DIM).transpose(0, 2, 1, 3)
    return shaped.reshape(seq_count, row_count, heads_here * HEAD_DIM)


def masked_scores(query_rows, key_rows, query_segs, key_segs):
    raw_scores = lax.dot_general(
        query_rows, key_rows, (((1,), (1,)), ((), ())), preferred_element_type=jnp.float32
    ) * HEAD_DIM ** (-0.5)
    return jnp.where(query_segs[:, None] == key_segs[None, :], raw_scores, masked_value)


def attend(pieces):
    query_rows, key_rows, value_rows, query_segs, key_segs = pieces
    scores = masked_scores(query_rows, key_rows, query_segs, key_segs)
    highest = jnp.max(scores, axis=1, keepdims=True)
    weights = jnp.exp(scores - highest)
    totals = jnp.sum(weights, axis=1, keepdims=True)
    softmax_rows = (weights / totals).astype(jnp.bfloat16)
    attended = jnp.dot(softmax_rows, value_rows, preferred_element_type=jnp.float32)
    return (attended, (highest + jnp.log(totals))[:, 0])


def attend_back(pieces):
    query_rows, key_rows, value_rows, grad_rows, log_totals, deltas, query_segs, key_segs = pieces
    scores = masked_scores(query_rows, key_rows, query_segs, key_segs)
    softmax_rows = jnp.exp(scores - log_totals[:, None])
    grad_softmax = lax.dot_general(
        grad_rows, value_rows, (((1,), (1,)), ((), ())), preferred_element_type=jnp.float32
    )
    grad_scores = (softmax_rows * (grad_softmax - deltas[:, None])).astype(jnp.bfloat16)
    score_scale = HEAD_DIM ** (-0.5)
    grad_query = jnp.dot(grad_scores, key_rows, preferred_element_type=jnp.float32) * score_scale
    grad_keys = (
        lax.dot_general(
            grad_scores, query_rows, (((0,), (0,)), ((), ())), preferred_element_type=jnp.float32
        )
        * score_scale
    )
    grad_values = lax.dot_general(
        softmax_rows.astype(jnp.bfloat16),
        grad_rows,
        (((0,), (0,)), ((), ())),
        preferred_element_type=jnp.float32,
    )
    return (grad_query, grad_keys, grad_values)


def norm_forward(resid, gain, shift):
    row_mean = jnp.mean(resid, axis=2, keepdims=True)
    spread = jnp.mean(resid * resid, axis=2, keepdims=True) - row_mean * row_mean
    inverse = lax.rsqrt(spread + epsilon)
    normed = (resid - row_mean) * inverse
    return (normed * gain + shift, normed, inverse)


def norm_backward(upstream, normed, inverse, gain):
    scaled = upstream * gain
    first_mean = jnp.mean(scaled, axis=2, keepdims=True)
    second_mean = jnp.mean(scaled * normed, axis=2, keepdims=True)
    back_term = inverse * (scaled - first_mean - normed * second_mean)
    return (back_term, jnp.sum(upstream * normed, axis=(0, 1)), jnp.sum(upstream, axis=(0, 1)))


def token_sum(tensor):
    return jnp.sum(tensor.astype(jnp.float32), axis=(0, 1))


def per_device(
    inputs,
    segments,
    query_weight,
    query_bias,
    key_weight,
    value_weight,
    value_bias,
    output_weight,
    output_bias,
    first_gain,
    first_shift,
    expand_weight,
    expand_bias,
    contract_weight,
    contract_bias,
    second_gain,
    second_shift,
    cotangent,
):
    seq_count, rows_here, _ = inputs.shape
    ctx_rows = rows_here * lax.axis_size("tp")
    heads_here = query_weight.shape[1] // HEAD_DIM
    own_segments = lax.dynamic_slice_in_dim(segments, lax.axis_index("ctx") * ctx_rows, ctx_rows, 1)
    query_segs = jnp.repeat(own_segments, heads_here, axis=0)
    key_segs = jnp.repeat(segments, heads_here, axis=0)
    front_set, back_set = fetch_weights(
        query_weight, key_weight, value_weight, expand_weight, output_weight, contract_weight
    )
    query_full, key_full, value_full, expand_full = front_set
    output_full, contract_full = back_set
    inputs_whole = whole_rows(inputs)
    query_low = (
        jnp.einsum("scd,de->sce", inputs_whole, query_full, preferred_element_type=jnp.float32)
        + query_bias
    ).astype(jnp.bfloat16)
    keys_low = jnp.einsum(
        "scd,de->sce", inputs_whole, key_full, preferred_element_type=jnp.float32
    ).astype(jnp.bfloat16)
    values_low = (
        jnp.einsum("scd,de->sce", inputs_whole, value_full, preferred_element_type=jnp.float32)
        + value_bias
    ).astype(jnp.bfloat16)
    keys_all, values_all = fetch_blocks(keys_low, values_low)
    query_items = to_items(query_low)
    attended_items, log_totals = lax.map(
        attend, (query_items, to_items(keys_all), to_items(values_all), query_segs, key_segs)
    )
    attended = from_items(attended_items, seq_count)
    attended_low = attended.astype(jnp.bfloat16)
    branch = (
        feature_sum(
            jnp.einsum("sce,ed->scd", attended_low, output_full, preferred_element_type=jnp.float32)
        )
        + output_bias
    )
    middle, middle_normed, middle_inverse = norm_forward(
        inputs.astype(jnp.float32) + branch, first_gain, first_shift
    )
    middle_whole = whole_rows(middle.astype(jnp.bfloat16))
    preact = (
        jnp.einsum("scd,df->scf", middle_whole, expand_full, preferred_element_type=jnp.float32)
        + expand_bias
    )
    active, gelu_pull = jax.vjp(exact_gelu, preact)
    active_low = active.astype(jnp.bfloat16)
    feedforward = (
        feature_sum(
            jnp.einsum("scf,fd->scd", active_low, contract_full, preferred_element_type=jnp.float32)
        )
        + contract_bias
    )
    outputs, final_normed, final_inverse = norm_forward(
        middle + feedforward, second_gain, second_shift
    )
    front_use, back_use = fetch_weights(
        query_weight, key_weight, value_weight, expand_weight, output_weight, contract_weight
    )
    keys_use, values_use = fetch_blocks(keys_low, values_low)
    query_use, key_use, value_use, expand_use = front_use
    output_use, contract_use = back_use
    final_grad, second_gain_grad, second_shift_grad = norm_backward(
        cotangent.astype(jnp.float32), final_normed, final_inverse, second_gain
    )
    feed_grad = final_grad.astype(jnp.bfloat16)
    contract_bias_grad = token_sum(feed_grad)
    feed_whole = whole_rows(feed_grad)
    contract_part = jnp.einsum(
        "scf,scd->fd", active_low, feed_whole, preferred_element_type=jnp.float32
    )
    active_grad = jnp.einsum(
        "scd,fd->scf", feed_whole, contract_use, preferred_element_type=jnp.float32
    )
    preact_grad = gelu_pull(active_grad)[0].astype(jnp.bfloat16)
    expand_bias_grad = token_sum(preact_grad)
    expand_part = jnp.einsum(
        "scd,scf->df", middle_whole, preact_grad, preferred_element_type=jnp.float32
    )
    middle_grad = final_grad + feature_sum(
        jnp.einsum("scf,df->scd", preact_grad, expand_use, preferred_element_type=jnp.float32)
    )
    resid_grad, first_gain_grad, first_shift_grad = norm_backward(
        middle_grad, middle_normed, middle_inverse, first_gain
    )
    branch_grad = resid_grad.astype(jnp.bfloat16)
    output_bias_grad = token_sum(branch_grad)
    branch_whole = whole_rows(branch_grad)
    output_part = jnp.einsum(
        "sce,scd->ed", attended_low, branch_whole, preferred_element_type=jnp.float32
    )
    attended_grad = jnp.einsum(
        "scd,ed->sce", branch_whole, output_use, preferred_element_type=jnp.float32
    ).astype(jnp.bfloat16)
    deltas = jnp.sum(
        (attended_grad.astype(jnp.float32) * attended).reshape(
            seq_count, ctx_rows, heads_here, HEAD_DIM
        ),
        axis=3,
    ).transpose(0, 2, 1)
    delta_items = deltas.reshape(seq_count * heads_here, ctx_rows)
    grad_items = to_items(attended_grad)
    query_back, keys_part, values_part = lax.map(
        attend_back,
        (
            query_items,
            to_items(keys_use),
            to_items(values_use),
            grad_items,
            log_totals,
            delta_items,
            query_segs,
            key_segs,
        ),
    )
    keys_grad, values_grad = (
        lax.psum_scatter(
            from_items(keys_part, seq_count).astype(jnp.bfloat16),
            "ctx",
            scatter_dimension=1,
            tiled=True,
        ).astype(jnp.float32),
        lax.psum_scatter(
            from_items(values_part, seq_count).astype(jnp.bfloat16),
            "ctx",
            scatter_dimension=1,
            tiled=True,
        ).astype(jnp.float32),
    )
    query_grad = from_items(query_back, seq_count).astype(jnp.bfloat16)
    keys_grad_low = keys_grad.astype(jnp.bfloat16)
    values_grad_low = values_grad.astype(jnp.bfloat16)
    query_bias_grad = token_sum(query_grad)
    value_bias_grad = token_sum(values_grad_low)
    query_part = jnp.einsum(
        "scd,sce->de", inputs_whole, query_grad, preferred_element_type=jnp.float32
    )
    key_part = jnp.einsum(
        "scd,sce->de", inputs_whole, keys_grad_low, preferred_element_type=jnp.float32
    )
    value_part = jnp.einsum(
        "scd,sce->de", inputs_whole, values_grad_low, preferred_element_type=jnp.float32
    )
    input_terms = (
        jnp.einsum("sce,de->scd", query_grad, query_use, preferred_element_type=jnp.float32)
        + jnp.einsum("sce,de->scd", keys_grad_low, key_use, preferred_element_type=jnp.float32)
        + jnp.einsum("sce,de->scd", values_grad_low, value_use, preferred_element_type=jnp.float32)
    )
    input_grad = (resid_grad + feature_sum(input_terms)).astype(jnp.bfloat16)
    query_weight_grad, key_weight_grad, value_weight_grad, expand_weight_grad = in_one_piece(
        (
            query_part.astype(jnp.bfloat16),
            key_part.astype(jnp.bfloat16),
            value_part.astype(jnp.bfloat16),
            expand_part.astype(jnp.bfloat16),
        ),
        ("fsdp", "ctx"),
        0,
        1,
    )
    output_weight_grad, contract_weight_grad = in_one_piece(
        (output_part.astype(jnp.bfloat16), contract_part.astype(jnp.bfloat16)),
        ("fsdp", "ctx"),
        1,
        0,
    )
    column_sums = lax.psum((query_bias_grad, value_bias_grad, expand_bias_grad), ("fsdp", "ctx"))
    whole_sums = lax.psum(
        (
            output_bias_grad,
            first_gain_grad,
            first_shift_grad,
            contract_bias_grad,
            second_gain_grad,
            second_shift_grad,
        ),
        ("fsdp", "ctx", "tp"),
    )
    return (
        outputs.astype(jnp.bfloat16),
        input_grad,
        query_weight_grad,
        column_sums[0],
        key_weight_grad,
        value_weight_grad,
        column_sums[1],
        output_weight_grad,
        whole_sums[0],
        whole_sums[1],
        whole_sums[2],
        expand_weight_grad,
        column_sums[2],
        contract_weight_grad,
        whole_sums[3],
        whole_sums[4],
        whole_sums[5],
    )


def solution(mesh):
    placed = (
        P("fsdp", ("ctx", "tp"), None),
        P("fsdp", None),
        P(("fsdp", "ctx"), "tp"),
        P("tp"),
        P(("fsdp", "ctx"), "tp"),
        P(("fsdp", "ctx"), "tp"),
        P("tp"),
        P("tp", ("fsdp", "ctx")),
        P(),
        P(),
        P(),
        P(("fsdp", "ctx"), "tp"),
        P("tp"),
        P("tp", ("fsdp", "ctx")),
        P(),
        P(),
        P(),
        P("fsdp", ("ctx", "tp"), None),
    )
    return jax.shard_map(
        per_device,
        mesh=mesh,
        in_specs=placed,
        out_specs=(
            P("fsdp", ("ctx", "tp"), None),
            P("fsdp", ("ctx", "tp"), None),
            P(("fsdp", "ctx"), "tp"),
            P("tp"),
            P(("fsdp", "ctx"), "tp"),
            P(("fsdp", "ctx"), "tp"),
            P("tp"),
            P("tp", ("fsdp", "ctx")),
            P(),
            P(),
            P(),
            P(("fsdp", "ctx"), "tp"),
            P("tp"),
            P("tp", ("fsdp", "ctx")),
            P(),
            P(),
            P(),
        ),
        check_vma=False,
    )
```

profile of v0, /device:TPU:0, one launch (start us, length us, event | category | flops | bytes accessed | tf_op | source)
XLA Modules:
  0.0 1107.1 jit_solution(9086204547020164236)
XLA Ops:
  8.8 11.3 %all_gather.48 = bf16[768,192]{1,0:T(8,128)(2,1)S(1)} all-gather(bf16[96,192]{1,0:T(8,128)(2,1)} %param.27), channel_id=1, replica_groups=mesh['fsdp'=2,'ctx'=4,'tp'=4] {'fsdp','ctx'}, dimensions={0}, use_global_device_ids=true | all-gather | bytes 331776 | tf_op jit(solution)/shard_map/all_gather | solution.py:52
  20.1 56.5 %all-gather.9.cloned.1.call-done = bf16[4,512,768]{2,1,0:T(8,128)(2,1)} async-done(((bf16[4,128,768]{2,1,0:T(8,128)(2,1)}), bf16[4,512,768]{2,1,0:T(8,128)(2,1)}) %all-gather.9.cloned.1.call-update) | async-done | bytes 3145744 | tf_op jit(solution)/shard_map/all_gather | solution.py:37
  80.8 9.9 all_gather.46
  100.1 10.6 all_gather.45
  110.7 10.4 all_gather.50
  126.6 4.5 copy.103
  131.2 9.1 all-gather.11.cloned.1.call-done
  142.9 4.5 copy.102
  147.4 137.5 %while.28 = (s32[]{:T(128)}, f32[12,512,64]{1,2,0:T(8,128)}, f32[12,512]{1,0:T(8,128)}, s32[12,512]{1,0:T(8,128)}, s32[12,2048]{1,0:T(8,128)}, /*index=5*/bf16[1...) while((s32[]{:T(128)}, f32[12,512,64]{1,2,0:T(8,128)}, ...), condition=%wide.region_3.4_spmd.clone, body=%wide.region_0.3_spmd.sunk.clone | while | flops 277872128 | bytes 30724220 | solution.py:191
  290.1 59.7 %reduce-scatter.7.cloned.1.call-done = bf16[4,128,768]{2,1,0:T(8,128)(2,1)} async-done(((bf16[4,512,768]{2,1,0:T(8,128)(2,1)}), bf16[4,128,768]{2,1,0:T(8,128)(2,1)}) %reduce-scatter.7.cloned.1.call-update) | async-done | bytes 786448 | tf_op jit(solution)/shard_map/reduce_scatter | solution.py:41
  354.6 62.7 %all-gather.15.cloned.1.call-done = bf16[4,512,768]{2,1,0:T(8,128)(2,1)} async-done(((bf16[4,128,768]{2,1,0:T(8,128)(2,1)}), bf16[4,512,768]{2,1,0:T(8,128)(2,1)}) %all-gather.15.cloned.1.call-update) | async-done | bytes 3145744 | tf_op jit(solution)/shard_map/all_gather | solution.py:37
  417.2 6.4 fusion.51
  426.3 15.6 %multiply_convert_fusion.1 = (bf16[4,512,768]{2,1,0:T(8,128)(2,1)}, f32[4,512,768]{2,1,0:T(8,128)}) fusion(f32[4,512,768]{2,1,0:T(8,128)S(1)} %get-tuple-element.315, f32[768]{0:T(1024)S(1)} %copy-done.37, u8[512,768]{1,0:T(8,128)(4,1)S(1)} %get-tuple-element.221, u8[512,768]{1,0:T(8,128)(4,1)S(1)} %get-tuple-element.220), kind=kLoop, calls=%fused_computation.62 | loop fusion | flops 111673344 | bytes 16518144 | tf_op jit(solution)/shard_map/convert_element_type | solution.py:211
  441.8 6.6 convolution_convert_fusion.2
  448.5 60.1 %reduce-scatter.9.cloned.1.call-done = bf16[4,128,768]{2,1,0:T(8,128)(2,1)} async-done(((bf16[4,512,768]{2,1,0:T(8,128)(2,1)}), bf16[4,128,768]{2,1,0:T(8,128)(2,1)}) %reduce-scatter.9.cloned.1.call-update) | async-done | bytes 786448 | tf_op jit(solution)/shard_map/reduce_scatter | solution.py:41
  516.6 63.0 %all-gather.21.cloned.1.call-done = bf16[4,512,768]{2,1,0:T(8,128)(2,1)} async-done(((bf16[4,128,768]{2,1,0:T(8,128)(2,1)}), bf16[4,512,768]{2,1,0:T(8,128)(2,1)}) %all-gather.21.cloned.1.call-update) | async-done | bytes 3145744 | tf_op jit(solution)/shard_map/all_gather | solution.py:37
  579.6 11.1 convert_reduce_fusion
  596.4 59.1 %reduce-scatter.11.cloned.1.call-done = bf16[4,128,768]{2,1,0:T(8,128)(2,1)} async-done(((bf16[4,512,768]{2,1,0:T(8,128)(2,1)}), bf16[4,128,768]{2,1,0:T(8,128)(2,1)}) %reduce-scatter.11.cloned.1.call-update) | async-done | bytes 786448 | tf_op jit(solution)/shard_map/reduce_scatter | solution.py:41
  655.5 4.2 multiply_reduce_fusion
  663.2 63.3 %all-gather.23.cloned.1.call-done = bf16[4,512,768]{2,1,0:T(8,128)(2,1)} async-done(((bf16[4,128,768]{2,1,0:T(8,128)(2,1)}), bf16[4,512,768]{2,1,0:T(8,128)(2,1)}) %all-gather.23.cloned.1.call-update) | async-done | bytes 3145744 | tf_op jit(solution)/shard_map/all_gather | solution.py:37
  737.0 149.8 %while.29 = (s32[]{:T(128)}, bf16[12,512,64]{1,2,0:T(8,128)(2,1)S(1)}, bf16[12,2048,64]{1,2,0:T(8,128)(2,1)}, bf16[12,2048,64]{1,2,0:T(8,128)(2,1)}, s32[12,512]...) while((s32[]{:T(128)}, ...), condition=%wide.region_17.18_spmd.clone, body=%wide.region_16.17_spmd.sunk.clone | while | flops 679641088 | bytes 22199424 | solution.py:267
  891.8 31.6 %reduce-scatter.13.cloned.1.call-done = bf16[4,512,192]{1,2,0:T(8,128)(2,1)} async-done(((bf16[4,2048,192]{1,2,0:T(8,128)(2,1)}), bf16[4,512,192]{1,2,0:T(8,128)(2,1)}) %reduce-scatter.13.cloned.1.call-update) | async-done | bytes 786448 | tf_op jit(solution)/shard_map/reduce_scatter | solution.py:281
  923.4 4.8 fusion.71
  928.3 35.4 %reduce-scatter.15.cloned.1.call-done = bf16[4,512,192]{1,2,0:T(8,128)(2,1)} async-done(((bf16[4,2048,192]{1,2,0:T(8,128)(2,1)}), bf16[4,512,192]{1,2,0:T(8,128)(2,1)}) %reduce-scatter.15.cloned.1.call-update) | async-done | bytes 786448 | tf_op jit(solution)/shard_map/reduce_scatter | solution.py:287
  963.7 7.6 add_convert_fusion
  971.3 5.7 bitcast_convert_fusion
  984.4 4.3 all-to-all-start.1
  995.2 4.1 copy.84
  999.4 9.4 all-to-all-done.1
  1008.8 4.4 all-to-all-start
  1013.2 60.9 %all-reduce = (f32[768]{0:T(1024)}, f32[768]{0:T(1024)}, f32[768]{0:T(1024)}, f32[768]{0:T(1024)}, f32[768]{0:T(1024)}, /*index=5*/f32[768]{0:T(1024)}) all-reduce(f32[768]{0:T(1024)S(1)} %copy-done.35, f32[768]{0:T(1024)S(1)} %copy-done.33, f32[768]{0:T(1024)S(1)} %copy-done.34, ...), channel_id=1, replica_groups=mesh['fsdp'=2,'ctx'=4,'tp'=4] {'fsdp','ctx','tp'}, use_global_device_ids=true, to_apply=%region_29.30 | all-reduce | flops 4608 | bytes 36864 | tf_op jit(solution)/shard_map/psum | solution.py:332
  1079.2 13.9 %all-reduce.1 = (f32[192]{0:T(256)}, f32[192]{0:T(256)}, f32[768]{0:T(1024)}) all-reduce(f32[192]{0:T(256)S(1)} %reduce_sum.211, f32[192]{0:T(256)S(1)} %convert_reduce_fusion.6, f32[768]{0:T(1024)S(1)} %copy-done.38), channel_id=1, replica_groups=mesh['fsdp'=2,'ctx'=4,'tp'=4] {'fsdp','ctx'}, use_global_device_ids=true, to_apply=%region_24.25 | all-reduce | flops 1152 | bytes 9216 | tf_op jit(solution)/shard_map/psum | solution.py:331
  (387 shorter events, 379.3 us)
Async XLA Ops:
  8.0 68.6 %all-gather.9.cloned.1.call-start = ((), (), s32[]{:S(2)}) async-start(), calls=%async_computation.8 | async-start | bytes 3932160 | tf_op jit(solution)/shard_map/all_gather | solution.py:37
  8.8 115.3 %all-gather.13.cloned.1.call-start = ((), (), s32[]{:S(2)}) async-start(), calls=%async_computation.10 | async-start | bytes 3932160 | tf_op jit(solution)/shard_map/all_gather | solution.py:65
  20.1 60.6 %copy-start.17 = (bf16[768,192]{1,0:T(8,128)(2,1)}, bf16[768,192]{1,0:T(8,128)(2,1)S(1)}, u32[]{:S(2)}) copy-start(bf16[768,192]{1,0:T(8,128)(2,1)S(1)} %all_gather.48) | copy-start | bytes 884740
  80.7 59.6 %all-gather.11.cloned.1.call-start = ((), (), s32[]{:S(2)}) async-start(), calls=%async_computation.9 | async-start | bytes 3932160 | tf_op jit(solution)/shard_map/all_gather | solution.py:64
  90.7 30.5 %copy-start.41 = (f32[192]{0:T(256)S(1)}, f32[192]{0:T(256)}, u32[]{:S(2)}) copy-start(f32[192]{0:T(256)} %param.25) | copy-start | bytes 2308
  92.7 257.1 %reduce-scatter.7.cloned.1.call-start = ((), (), s32[]{:S(2)}) async-start(), calls=%async_computation.11 | async-start | bytes 3932160 | tf_op jit(solution)/shard_map/reduce_scatter | solution.py:41
  147.4 139.1 %copy-start.7 = (bf16[192,768]{0,1:T(8,128)(2,1)S(1)}, bf16[192,768]{0,1:T(8,128)(2,1)}, u32[]{:S(2)}) copy-start(bf16[192,768]{0,1:T(8,128)(2,1)} %all_gather.50) | copy-start | bytes 884740
  286.5 63.3 %copy-start.1 = (bf16[4,128,768]{2,1,0:T(8,128)(2,1)S(1)}, bf16[4,128,768]{2,1,0:T(8,128)(2,1)}, u32[]{:S(2)}) copy-start(bf16[4,128,768]{2,1,0:T(8,128)(2,1)} %param.22) | copy-start | bytes 2359300
  286.5 63.3 %copy-start.20 = (f32[768]{0:T(1024)S(1)}, f32[768]{0:T(1024)}, u32[]{:S(2)}) copy-start(f32[768]{0:T(1024)} %param.30) | copy-start | bytes 9220
  289.2 62.2 %copy-start.21 = (f32[768]{0:T(1024)S(1)}, f32[768]{0:T(1024)}, u32[]{:S(2)}) copy-start(f32[768]{0:T(1024)} %param.31) | copy-start | bytes 9220
  289.2 62.2 %copy-start.36 = (f32[768]{0:T(1024)S(1)}, f32[768]{0:T(1024)}, u32[]{:S(2)}) copy-start(f32[768]{0:T(1024)} %param.32) | copy-start | bytes 9220
  289.3 128.0 %copy-start.37 = (f32[768]{0:T(1024)S(1)}, f32[768]{0:T(1024)}, u32[]{:S(2)}) copy-start(f32[768]{0:T(1024)} %param.34) | copy-start | bytes 9220
  289.3 65.3 %all-gather.17.cloned.1.call-start = ((), (), s32[]{:S(2)}) async-start(), calls=%async_computation.13 | async-start | bytes 1327104 | tf_op jit(solution)/shard_map/all_gather | solution.py:53
  289.8 127.4 %all-gather.15.cloned.1.call-start = ((), (), s32[]{:S(2)}) async-start(), calls=%async_computation.12 | async-start | bytes 3932160 | tf_op jit(solution)/shard_map/all_gather | solution.py:37
  353.9 87.9 %all-gather.19.cloned.1.call-start = ((), (), s32[]{:S(2)}) async-start(), calls=%async_computation.14 | async-start | bytes 1327104 | tf_op jit(solution)/shard_map/all_gather | solution.py:57
  354.5 154.1 %reduce-scatter.9.cloned.1.call-start = ((), (), s32[]{:S(2)}) async-start(), calls=%async_computation.15 | async-start | bytes 3932160 | tf_op jit(solution)/shard_map/reduce_scatter | solution.py:41
  448.4 60.2 %copy-start.2 = (bf16[4,128,768]{2,1,0:T(8,128)(2,1)S(1)}, bf16[4,128,768]{2,1,0:T(8,128)(2,1)}, u32[]{:S(2)}) copy-start(bf16[4,128,768]{2,1,0:T(8,128)(2,1)} %reduce-scatter.7.cloned.1.call-done) | copy-start | bytes 2359300
  448.5 131.1 %all-gather.21.cloned.1.call-start = ((), (), s32[]{:S(2)}) async-start(), calls=%async_computation.16 | async-start | bytes 3932160 | tf_op jit(solution)/shard_map/all_gather | solution.py:37
  516.3 139.2 %reduce-scatter.11.cloned.1.call-start = ((), (), s32[]{:S(2)}) async-start(), calls=%async_computation.17 | async-start | bytes 3932160 | tf_op jit(solution)/shard_map/reduce_scatter | solution.py:41
  596.4 130.1 %all-gather.23.cloned.1.call-start = ((), (), s32[]{:S(2)}) async-start(), calls=%async_computation.18 | async-start | bytes 3932160 | tf_op jit(solution)/shard_map/all_gather | solution.py:37
  659.7 66.8 %copy-start.8 = (bf16[192,768]{0,1:T(8,128)(2,1)S(1)}, bf16[192,768]{0,1:T(8,128)(2,1)}, u32[]{:S(2)}) copy-start(bf16[192,768]{0,1:T(8,128)(2,1)} %all_gather.50) | copy-start | bytes 884740
  659.7 70.0 %copy-start.24 = (f32[4,128]{1,0:T(4,128)}, f32[4,128]{1,0:T(4,128)S(1)}, u32[]{:S(2)}) copy-start(f32[4,128]{1,0:T(4,128)S(1)} %broadcast_multiply_fusion) | copy-start | bytes 6148
  659.7 70.0 %copy-start.26 = (f32[4,128]{1,0:T(4,128)}, f32[4,128]{1,0:T(4,128)S(1)}, u32[]{:S(2)}) copy-start(f32[4,128]{1,0:T(4,128)S(1)} %broadcast_multiply_fusion.1) | copy-start | bytes 6148
  663.0 260.4 %reduce-scatter.13.cloned.1.call-start = ((), (), s32[]{:S(2)}) async-start(), calls=%async_computation.19 | async-start | bytes 3932160 | tf_op jit(solution)/shard_map/reduce_scatter | solution.py:281
  886.9 76.8 %reduce-scatter.15.cloned.1.call-start = ((), (), s32[]{:S(2)}) async-start(), calls=%async_computation.20 | async-start | bytes 3932160 | tf_op jit(solution)/shard_map/reduce_scatter | solution.py:287
  887.7 209.0 %reduce-scatter.17.cloned.1.call-start = ((), (), s32[]{:S(2)}) async-start(), calls=%async_computation.21 | async-start | bytes 3932160 | tf_op jit(solution)/shard_map/reduce_scatter | solution.py:41
  891.8 71.9 %copy-start.18 = (bf16[768,192]{1,0:T(8,128)(2,1)S(1)}, bf16[768,192]{1,0:T(8,128)(2,1)}, u32[]{:S(2)}) copy-start(bf16[768,192]{1,0:T(8,128)(2,1)} %copy-done.17) | copy-start | bytes 884740
  984.4 24.4 %all-to-all-start.1 = ((bf16[8,960,96]{1,2,0:T(8,128)(2,1)}), bf16[8,960,96]{1,2,0:T(8,128)(2,1)}, u32[]{:S(2)}, u32[]{:S(2)}) async-start(bf16[8,960,96]{1,2,0:T(8,128)(2,1)} %bitcast.258), calls=%async_computation.7 | async-start | bytes 3145728 | tf_op jit(solution)/shard_map/all_to_all | solution.py:19
  1008.8 84.3 %all-to-all-start = ((bf16[8,96,1344]{2,1,0:T(8,128)(2,1)}), bf16[8,96,1344]{2,1,0:T(8,128)(2,1)}, u32[]{:S(2)}, u32[]{:S(2)}) async-start(bf16[8,96,1344]{2,1,0:T(8,128)(2,1)} %bitcast.255), calls=%async_computation.6 | async-start | bytes 4325376 | tf_op jit(solution)/shard_map/all_to_all | solution.py:19
  1013.2 66.0 %copy-start.38 = (f32[768]{0:T(1024)S(1)}, f32[768]{0:T(1024)}, u32[]{:S(2)}) copy-start(f32[768]{0:T(1024)} %get-tuple-element.316) | copy-start | bytes 9220
  1076.2 20.5 %copy-start.4 = (f32[4,128,768]{2,1,0:T(8,128)S(1)}, f32[4,128,768]{2,1,0:T(8,128)}, u32[]{:S(2)}) copy-start(f32[4,128,768]{2,1,0:T(8,128)} %copy-done.3) | copy-start | bytes 4718596
  1076.2 20.5 %copy-start.25 = (f32[4,128]{1,0:T(4,128)S(1)}, f32[4,128]{1,0:T(4,128)}, u32[]{:S(2)}) copy-start(f32[4,128]{1,0:T(4,128)} %copy-done.24) | copy-start | bytes 6148
  (39 other events, 217.0 us)
Sparse Core Ops, SparseCore 0:
  10.4 66.1 all-gather.8
  80.9 27.7 all-gather.12
  110.8 29.4 all-gather.10
  289.4 60.3 reduce-scatter.6
  663.1 63.2 all-gather.22
  887.0 36.3 reduce-scatter.12
  926.0 37.7 reduce-scatter.14
Sparse Core Ops, SparseCore 1:
  291.6 23.8 all-gather.16
  354.0 63.2 all-gather.14
  419.0 22.4 all-gather.18
  448.5 60.0 reduce-scatter.8
  516.4 63.1 all-gather.20
  596.4 59.0 reduce-scatter.10
  971.4 60.3 reduce-scatter.16
where the time goes:
time: 1120 us; the launch traced here: 1110 us
  waiting for transfers between devices  513 us (46%)
  matrix products  263 us (23%)
  local copies, waits for them, and re-layouts  128 us (11%)
  blocking collectives  117 us (10%)
  other arithmetic  59.3 us (5%)
  between operations  16.5 us (1%)
    all_gather x4, waiting for transfers between devices, whole_rows(): return lax.all_gather(tensor, 'tp', axis=1, tiled=True)  245 us
    reduce_scatter x4, waiting for transfers between devices, feature_sum(): lax.psum_scatter(tensor.astype(jnp.bfloat16), 'tp', scatter_dimension=1,...  179 us
    psum x1, blocking collectives, per_device(): lax.psum((output_bias_grad, first_gain_grad, first_shift_grad, contract_b...  60.9 us
    dot_general x24, matrix products, masked_scores(): lax.dot_general(query_rows, key_rows, (((1,), (1,)), ((), ())), preferred...  49.7 us
    dot_general x12, matrix products, attend(): jnp.dot(softmax_rows, value_rows, preferred_element_type=jnp.float32)  47.1 us
    dynamic_slice x48, local copies, waits for them, and re-layouts, per_device(): lax.map(attend, (query_items, to_items(keys_all), to_items(values_all), q...  37.8 us
    reduce_scatter x1, waiting for transfers between devices, per_device(): lax.psum_scatter(from_items(values_part, seq_count).astype(jnp.bfloat16),...  35.4 us
    reduce_scatter x1, waiting for transfers between devices, per_device(): lax.psum_scatter(from_items(keys_part, seq_count).astype(jnp.bfloat16), '...  31.6 us
  transfers between devices with their start and end apart: 16, of which 11 were waited for; matrix products, arithmetic and copies ran while one was open for 8% of the time, Pallas kernels for 0%

commit v1 on v0

--- a/solution.py
+++ b/solution.py
@@ -6,6 +6,21 @@
 HEAD_DIM = 64
 epsilon = 1e-05
 masked_value = -1e30
+
+
+def _review_pairs_all(matrix, out_dim):
+    prior, outcome_arr = (lax.axis_size("tp"), lax.axis_index("tp"))
+    vec_out, reply = (matrix, 1)
+    while reply < prior:
+        row_list = []
+        for t in range(prior):
+            row_list.append((t, t ^ reply))
+        big = lax.ppermute(vec_out, "tp", row_list)
+        b_now = jnp.concatenate([vec_out, big], axis=out_dim)
+        h_now = jnp.concatenate([big, vec_out], axis=out_dim)
+        vec_out = jnp.where(outcome_arr & reply == 0, b_now, h_now)
+        reply = 2 * reply
+    return vec_out
 
 
 def in_blocks(value, dim, count):
@@ -34,7 +49,7 @@
 
 
 def whole_rows(tensor):
-    return lax.all_gather(tensor, "tp", axis=1, tiled=True)
+    return _review_pairs_all(tensor, 1)
 
 
 def feature_sum(tensor):

time: 1120 us -> 1230 us (1.098)
  waiting for transfers between devices: 513 us -> 594 us
  starting transfers between devices: 10 us -> 26.7 us
    ppermute x0 -> x8, waiting for transfers between devices: none -> 330 us  [_review_pairs_all(): big = lax.ppermute(vec_out, 'tp', row_list)]
    all_gather x4 -> x0, waiting for transfers between devices: 245 us -> none  [whole_rows(): return lax.all_gather(tensor, 'tp', axis=1, tiled=True)]
    ppermute x0 -> x8, starting transfers between devices: none -> 16.8 us  [_review_pairs_all(): big = lax.ppermute(vec_out, 'tp', row_list)]
  transfers between devices with their start and end apart: 16 -> 20, of which waited for: 11 -> 16; matrix products, arithmetic and copies ran while one was open for 8% -> 8% of each run, Pallas kernels for 0% -> 0%
where the time goes in v1:
time: 1230 us; the launch traced here: 1220 us
  waiting for transfers between devices  594 us (48%)
  matrix products  267 us (22%)
  local copies, waits for them, and re-layouts  129 us (10%)
  blocking collectives  116 us (9%)
  other arithmetic  66.6 us (5%)
  starting transfers between devices  26.7 us (2%)
  between operations  16.8 us (1%)
    ppermute x8, waiting for transfers between devices, _review_pairs_all(): big = lax.ppermute(vec_out, 'tp', row_list)  330 us
    reduce_scatter x4, waiting for transfers between devices, feature_sum(): lax.psum_scatter(tensor.astype(jnp.bfloat16), 'tp', scatter_dimension=1,...  181 us
    psum x1, blocking collectives, per_device(): lax.psum((output_bias_grad, first_gain_grad, first_shift_grad, contract_b...  60.9 us
    dot_general x24, matrix products, masked_scores(): lax.dot_general(query_rows, key_rows, (((1,), (1,)), ((), ())), preferred...  48.8 us
    dot_general x12, matrix products, attend(): jnp.dot(softmax_rows, value_rows, preferred_element_type=jnp.float32)  39.2 us
    dynamic_slice x48, local copies, waits for them, and re-layouts, per_device(): lax.map(attend, (query_items, to_items(keys_all), to_items(values_all), q...  37.8 us
    reduce_scatter x1, waiting for transfers between devices, per_device(): lax.psum_scatter(from_items(values_part, seq_count).astype(jnp.bfloat16),...  35.5 us
    reduce_scatter x1, waiting for transfers between devices, per_device(): lax.psum_scatter(from_items(keys_part, seq_count).astype(jnp.bfloat16), '...  33.2 us
  transfers between devices with their start and end apart: 20, of which 16 were waited for; matrix products, arithmetic and copies ran while one was open for 8% of the time, Pallas kernels for 0%

profile of v1, /device:TPU:0, one launch (start us, length us, event | category | flops | bytes accessed | tf_op | source)
XLA Modules:
  0.0 1216.7 jit_solution(10606072545417409633)
XLA Ops:
  11.2 17.8 %collective-permute-done = bf16[4,128,768]{2,1,0:T(8,128)(2,1)S(1)} collective-permute-done((bf16[4,128,768]{2,1,0:T(8,128)(2,1)}, bf16[4,128,768]{2,1,0:T(8,128)(2,1)S(1)}, u32[]{:S(2)}, u32[]{:S(2)}) %collective-permute-start) | collective-permute-done | bytes 786464 | tf_op jit(solution)/shard_map/ppermute | solution.py:18
  33.7 9.6 all_gather.35
  43.2 57.9 %collective-permute-done.1 = bf16[4,256,768]{2,1,0:T(8,128)(2,1)} collective-permute-done((bf16[4,256,768]{2,1,0:T(8,128)(2,1)S(1)}, bf16[4,256,768]{2,1,0:T(8,128)(2,1)}, u32[]{:S(2)}, u32[]{:S(2)}) %collective-permute-start.1) | collective-permute-done | bytes 1572896 | tf_op jit(solution)/shard_map/ppermute | solution.py:18
  105.2 9.5 all_gather.33
  121.1 11.5 all_gather.32
  132.6 11.0 all_gather.37
  153.8 6.6 copy.103
  160.4 6.7 all-gather.5.cloned.1.call-done
  171.2 6.6 copy.102
  177.8 129.3 %while.28 = (s32[]{:T(128)}, f32[12,512,64]{1,2,0:T(8,128)S(1)}, f32[12,512]{1,0:T(8,128)}, s32[12,512]{1,0:T(8,128)}, s32[12,2048]{1,0:T(8,128)}, /*index=5*/bf...) while((s32[]{:T(128)}, f32[12,512,64]{1,2,0:T(8,128)S(1)}, ...), condition=%wide.region_3.4_spmd.clone, body=%wide.region_0.3_spmd.sunk.clone | while | flops 277872128 | bytes 30724220 | solution.py:206
  313.1 60.5 %reduce-scatter.7.cloned.1.call-done = bf16[4,128,768]{2,1,0:T(8,128)(2,1)} async-done(((bf16[4,512,768]{2,1,0:T(8,128)(2,1)}), bf16[4,128,768]{2,1,0:T(8,128)(2,1)}) %reduce-scatter.7.cloned.1.call-update) | async-done | bytes 786448 | tf_op jit(solution)/shard_map/reduce_scatter | solution.py:56
  377.8 18.1 %collective-permute-done.2 = bf16[4,128,768]{2,1,0:T(8,128)(2,1)} collective-permute-done((bf16[4,128,768]{2,1,0:T(8,128)(2,1)S(1)}, bf16[4,128,768]{2,1,0:T(8,128)(2,1)}, u32[]{:S(2)}, u32[]{:S(2)}) %collective-permute-start.2) | collective-permute-done | bytes 786464 | tf_op jit(solution)/shard_map/ppermute | solution.py:18
  402.2 65.8 %collective-permute-done.3 = bf16[4,256,768]{2,1,0:T(8,128)(2,1)} collective-permute-done((bf16[4,256,768]{2,1,0:T(8,128)(2,1)S(1)}, bf16[4,256,768]{2,1,0:T(8,128)(2,1)}, u32[]{:S(2)}, u32[]{:S(2)}) %collective-permute-start.3) | collective-permute-done | bytes 1572896 | tf_op jit(solution)/shard_map/ppermute | solution.py:18
  468.0 6.5 fusion.51
  477.1 16.3 %multiply_convert_fusion.1 = (bf16[4,512,768]{2,1,0:T(8,128)(2,1)}, f32[4,512,768]{2,1,0:T(8,128)}) fusion(f32[4,512,768]{2,1,0:T(8,128)S(1)} %get-tuple-element.315, f32[768]{0:T(1024)} %param.34, u8[512,768]{1,0:T(8,128)(4,1)S(1)} %get-tuple-element.221, u8[512,768]{1,0:T(8,128)(4,1)S(1)} %get-tuple-element.220), kind=kLoop, calls=%fused_computation.62 | loop fusion | flops 111673344 | bytes 16518144 | tf_op jit(solution)/shard_map/convert_element_type | solution.py:226
  493.4 6.6 convolution_convert_fusion.2
  500.1 60.4 %reduce-scatter.9.cloned.1.call-done = bf16[4,128,768]{2,1,0:T(8,128)(2,1)} async-done(((bf16[4,512,768]{2,1,0:T(8,128)(2,1)}), bf16[4,128,768]{2,1,0:T(8,128)(2,1)}) %reduce-scatter.9.cloned.1.call-update) | async-done | bytes 786448 | tf_op jit(solution)/shard_map/reduce_scatter | solution.py:56
  568.7 18.0 %collective-permute-done.4 = bf16[4,128,768]{2,1,0:T(8,128)(2,1)S(1)} collective-permute-done((bf16[4,128,768]{2,1,0:T(8,128)(2,1)S(1)}, bf16[4,128,768]{2,1,0:T(8,128)(2,1)S(1)}, u32[]{:S(2)}, u32[]{:S(2)}) %collective-permute-start.4) | collective-permute-done | bytes 786464 | tf_op jit(solution)/shard_map/ppermute | solution.py:18
  590.1 67.2 %collective-permute-done.5 = bf16[4,256,768]{2,1,0:T(8,128)(2,1)S(1)} collective-permute-done((bf16[4,256,768]{2,1,0:T(8,128)(2,1)S(1)}, bf16[4,256,768]{2,1,0:T(8,128)(2,1)S(1)}, u32[]{:S(2)}, u32[]{:S(2)}) %collective-permute-start.5) | collective-permute-done | bytes 1572896 | tf_op jit(solution)/shard_map/ppermute | solution.py:18
  657.3 7.4 convert_reduce_fusion
  670.7 60.3 %reduce-scatter.11.cloned.1.call-done = bf16[4,128,768]{2,1,0:T(8,128)(2,1)} async-done(((bf16[4,512,768]{2,1,0:T(8,128)(2,1)}), bf16[4,128,768]{2,1,0:T(8,128)(2,1)}) %reduce-scatter.11.cloned.1.call-update) | async-done | bytes 786448 | tf_op jit(solution)/shard_map/reduce_scatter | solution.py:56
  738.6 18.0 %collective-permute-done.6 = bf16[4,128,768]{2,1,0:T(8,128)(2,1)S(1)} collective-permute-done((bf16[4,128,768]{2,1,0:T(8,128)(2,1)S(1)}, bf16[4,128,768]{2,1,0:T(8,128)(2,1)S(1)}, u32[]{:S(2)}, u32[]{:S(2)}) %collective-permute-start.6) | collective-permute-done | bytes 786464 | tf_op jit(solution)/shard_map/ppermute | solution.py:18
  761.2 67.4 %collective-permute-done.7 = bf16[4,256,768]{2,1,0:T(8,128)(2,1)} collective-permute-done((bf16[4,256,768]{2,1,0:T(8,128)(2,1)}, bf16[4,256,768]{2,1,0:T(8,128)(2,1)}, u32[]{:S(2)}, u32[]{:S(2)}) %collective-permute-start.7) | collective-permute-done | bytes 1572896 | tf_op jit(solution)/shard_map/ppermute | solution.py:18
  840.2 149.7 %while.29 = (s32[]{:T(128)}, bf16[12,512,64]{1,2,0:T(8,128)(2,1)S(1)}, bf16[12,2048,64]{1,2,0:T(8,128)(2,1)}, bf16[12,2048,64]{1,2,0:T(8,128)(2,1)}, s32[12,512]...) while((s32[]{:T(128)}, ...), condition=%wide.region_17.18_spmd.clone, body=%wide.region_16.17_spmd.sunk.clone | while | flops 679641088 | bytes 22199424 | solution.py:282
  994.7 33.2 %reduce-scatter.13.cloned.1.call-done = bf16[4,512,192]{1,2,0:T(8,128)(2,1)} async-done(((bf16[4,2048,192]{1,2,0:T(8,128)(2,1)}), bf16[4,512,192]{1,2,0:T(8,128)(2,1)}) %reduce-scatter.13.cloned.1.call-update) | async-done | bytes 786448 | tf_op jit(solution)/shard_map/reduce_scatter | solution.py:296
  1028.0 4.8 fusion.68
  1032.8 35.5 %reduce-scatter.15.cloned.1.call-done = bf16[4,512,192]{1,2,0:T(8,128)(2,1)} async-done(((bf16[4,2048,192]{1,2,0:T(8,128)(2,1)}), bf16[4,512,192]{1,2,0:T(8,128)(2,1)}) %reduce-scatter.15.cloned.1.call-update) | async-done | bytes 786448 | tf_op jit(solution)/shard_map/reduce_scatter | solution.py:302
  1068.3 7.5 add_convert_fusion
  1075.9 6.8 bitcast_convert_fusion.1
  1093.4 4.6 all-to-all-start.1
  1122.5 60.9 %all-reduce = (f32[768]{0:T(1024)}, f32[768]{0:T(1024)}, f32[768]{0:T(1024)}, f32[768]{0:T(1024)}, f32[768]{0:T(1024)}, /*index=5*/f32[768]{0:T(1024)}) all-reduce(f32[768]{0:T(1024)S(1)} %copy-done.44, f32[768]{0:T(1024)S(1)} %copy-done.42, f32[768]{0:T(1024)S(1)} %copy-done.43, ...), channel_id=1, replica_groups=mesh['fsdp'=2,'ctx'=4,'tp'=4] {'fsdp','ctx','tp'}, use_global_device_ids=true, to_apply=%region_29.30 | all-reduce | flops 4608 | bytes 36864 | tf_op jit(solution)/shard_map/psum | solution.py:347
  1188.4 13.9 %all-reduce.1 = (f32[192]{0:T(256)}, f32[192]{0:T(256)}, f32[768]{0:T(1024)}) all-reduce(f32[192]{0:T(256)S(1)} %reduce_sum.211, f32[192]{0:T(256)S(1)} %convert_reduce_fusion.6, f32[768]{0:T(1024)S(1)} %copy-done.47), channel_id=1, replica_groups=mesh['fsdp'=2,'ctx'=4,'tp'=4] {'fsdp','ctx'}, use_global_device_ids=true, to_apply=%region_24.25 | all-reduce | flops 1152 | bytes 9216 | tf_op jit(solution)/shard_map/psum | solution.py:346
  (420 shorter events, 422.2 us)
Async XLA Ops:
  8.0 93.2 %copy-start.51 = (f32[192]{0:T(256)S(1)}, f32[192]{0:T(256)}, u32[]{:S(2)}) copy-start(f32[192]{0:T(256)} %param.28) | copy-start | bytes 2308
  8.0 141.7 %all-gather.7.cloned.1.call-start = ((), (), s32[]{:S(2)}) async-start(), calls=%async_computation.9 | async-start | bytes 3932160 | tf_op jit(solution)/shard_map/all_gather | solution.py:80
  8.1 20.9 %collective-permute-start = (bf16[4,128,768]{2,1,0:T(8,128)(2,1)}, bf16[4,128,768]{2,1,0:T(8,128)(2,1)S(1)}, u32[]{:S(2)}, u32[]{:S(2)}) collective-permute-start(bf16[4,128,768]{2,1,0:T(8,128)(2,1)} %param.22), channel_id=1, source_target_pairs={{0,1},{1,0},{2,3},{3,2},{4,5},{5,4},{6,7},{7,6},{8,9},{9,8},{10,11... | collective-permute-start | bytes 2359304 | tf_op jit(solution)/shard_map/ppermute | solution.py:18
  30.8 112.8 %copy-start.17 = (bf16[4,256,768]{2,1,0:T(8,128)(2,1)}, bf16[4,256,768]{2,1,0:T(8,128)(2,1)S(1)}, u32[]{:S(2)}) copy-start(bf16[4,256,768]{2,1,0:T(8,128)(2,1)S(1)} %maximum_select_fusion.4) | copy-start | bytes 4718596
  30.8 70.3 %collective-permute-start.1 = (bf16[4,256,768]{2,1,0:T(8,128)(2,1)S(1)}, bf16[4,256,768]{2,1,0:T(8,128)(2,1)}, u32[]{:S(2)}, u32[]{:S(2)}) collective-permute-start(bf16[4,256,768]{2,1,0:T(8,128)(2,1)S(1)} %maximum_select_fusion.4), channel_id=1, source_target_pairs={{0,2},{1,3},{2,0},{3,1},{4,6},{5,7},{6,4},{7,5},{8,10},{9,11},{10,... | collective-permute-start | bytes 4718600 | tf_op jit(solution)/shard_map/ppermute | solution.py:18
  105.2 61.9 %all-gather.5.cloned.1.call-start = ((), (), s32[]{:S(2)}) async-start(), calls=%async_computation.8 | async-start | bytes 3932160 | tf_op jit(solution)/shard_map/all_gather | solution.py:79
  118.9 254.7 %reduce-scatter.7.cloned.1.call-start = ((), (), s32[]{:S(2)}) async-start(), calls=%async_computation.10 | async-start | bytes 3932160 | tf_op jit(solution)/shard_map/reduce_scatter | solution.py:56
  313.0 89.1 %all-gather.9.cloned.1.call-start = ((), (), s32[]{:S(2)}) async-start(), calls=%async_computation.11 | async-start | bytes 1327104 | tf_op jit(solution)/shard_map/all_gather | solution.py:68
  376.8 19.1 %collective-permute-start.2 = (bf16[4,128,768]{2,1,0:T(8,128)(2,1)S(1)}, bf16[4,128,768]{2,1,0:T(8,128)(2,1)}, u32[]{:S(2)}, u32[]{:S(2)}) collective-permute-start(bf16[4,128,768]{2,1,0:T(8,128)(2,1)S(1)} %fusion.52), channel_id=1, source_target_pairs={{0,1},{1,0},{2,3},{3,2},{4,5},{5,4},{6,7},{7,6},{8,9},{9,8},{10,11... | collective-permute-start | bytes 2359304 | tf_op jit(solution)/shard_map/ppermute | solution.py:18
  377.8 115.7 %all-gather.11.cloned.1.call-start = ((), (), s32[]{:S(2)}) async-start(), calls=%async_computation.12 | async-start | bytes 1327104 | tf_op jit(solution)/shard_map/all_gather | solution.py:72
  397.8 76.7 %copy-start.19 = (bf16[4,256,768]{2,1,0:T(8,128)(2,1)}, bf16[4,256,768]{2,1,0:T(8,128)(2,1)S(1)}, u32[]{:S(2)}) copy-start(bf16[4,256,768]{2,1,0:T(8,128)(2,1)S(1)} %maximum_select_fusion.5) | copy-start | bytes 4718596
  397.8 70.2 %collective-permute-start.3 = (bf16[4,256,768]{2,1,0:T(8,128)(2,1)S(1)}, bf16[4,256,768]{2,1,0:T(8,128)(2,1)}, u32[]{:S(2)}, u32[]{:S(2)}) collective-permute-start(bf16[4,256,768]{2,1,0:T(8,128)(2,1)S(1)} %maximum_select_fusion.5), channel_id=1, source_target_pairs={{0,2},{1,3},{2,0},{3,1},{4,6},{5,7},{6,4},{7,5},{8,10},{9,11},{10,... | collective-permute-start | bytes 4718600 | tf_op jit(solution)/shard_map/ppermute | solution.py:18
  400.5 160.0 %reduce-scatter.9.cloned.1.call-start = ((), (), s32[]{:S(2)}) async-start(), calls=%async_computation.13 | async-start | bytes 3932160 | tf_op jit(solution)/shard_map/reduce_scatter | solution.py:56
  500.1 231.0 %reduce-scatter.11.cloned.1.call-start = ((), (), s32[]{:S(2)}) async-start(), calls=%async_computation.14 | async-start | bytes 3932160 | tf_op jit(solution)/shard_map/reduce_scatter | solution.py:56
  560.5 96.7 %slice-start = ((s8[6291456]{0:T(1024)(128)(4,1)}), s8[4194304]{0:T(1024)(128)(4,1)S(1)}, s32[]{:S(2)}) async-start(s8[6291456]{0:T(1024)(128)(4,1)} %bitcast.234), calls=%async_computation.18 | async-start | bytes 8388608
  562.7 94.6 %slice-start.1 = ((s8[6291456]{0:T(1024)(128)(4,1)}), s8[2097152]{0:T(1024)(128)(4,1)S(1)}, s32[]{:S(2)}) async-start(s8[6291456]{0:T(1024)(128)(4,1)} %bitcast.234), calls=%async_computation.19 | async-start | bytes 4194304
  565.3 92.0 %copy-start.6 = (f32[4,512,768]{2,1,0:T(8,128)S(1)}, f32[4,512,768]{2,1,0:T(8,128)}, u32[]{:S(2)}) copy-start(f32[4,512,768]{2,1,0:T(8,128)} %get-tuple-element.290) | copy-start | bytes 18874372
  565.3 92.0 %copy-start.46 = (f32[768]{0:T(1024)S(1)}, f32[768]{0:T(1024)}, u32[]{:S(2)}) copy-start(f32[768]{0:T(1024)} %param.34) | copy-start | bytes 9220
  567.8 18.9 %collective-permute-start.4 = (bf16[4,128,768]{2,1,0:T(8,128)(2,1)S(1)}, bf16[4,128,768]{2,1,0:T(8,128)(2,1)S(1)}, u32[]{:S(2)}, u32[]{:S(2)}) collective-permute-start(bf16[4,128,768]{2,1,0:T(8,128)(2,1)S(1)} %get-tuple-element.284), channel_id=1, source_target_pairs={{0,1},{1,0},{2,3},{3,2},{4,5},{5,4},{6,7},{7,6},{8,9},{9,8},{10,11... | collective-permute-start | bytes 2359304 | tf_op jit(solution)/shard_map/ppermute | solution.py:18
  587.3 77.4 %copy-start.20 = (bf16[4,256,768]{2,1,0:T(8,128)(2,1)}, bf16[4,256,768]{2,1,0:T(8,128)(2,1)S(1)}, u32[]{:S(2)}) copy-start(bf16[4,256,768]{2,1,0:T(8,128)(2,1)S(1)} %maximum_select_fusion.6) | copy-start | bytes 4718596
  587.3 69.9 %collective-permute-start.5 = (bf16[4,256,768]{2,1,0:T(8,128)(2,1)S(1)}, bf16[4,256,768]{2,1,0:T(8,128)(2,1)S(1)}, u32[]{:S(2)}, u32[]{:S(2)}) collective-permute-start(bf16[4,256,768]{2,1,0:T(8,128)(2,1)S(1)} %maximum_select_fusion.6), channel_id=1, source_target_pairs={{0,2},{1,3},{2,0},{3,1},{4,6},{5,7},{6,4},{7,5},{8,10},{9,11},{10,... | collective-permute-start | bytes 4718600 | tf_op jit(solution)/shard_map/ppermute | solution.py:18
  670.4 357.5 %reduce-scatter.13.cloned.1.call-start = ((), (), s32[]{:S(2)}) async-start(), calls=%async_computation.15 | async-start | bytes 3932160 | tf_op jit(solution)/shard_map/reduce_scatter | solution.py:296
  736.4 92.2 %copy-start.16 = (bf16[192,768]{0,1:T(8,128)(2,1)S(1)}, bf16[192,768]{0,1:T(8,128)(2,1)}, u32[]{:S(2)}) copy-start(bf16[192,768]{0,1:T(8,128)(2,1)} %all_gather.37) | copy-start | bytes 884740
  737.7 18.9 %collective-permute-start.6 = (bf16[4,128,768]{2,1,0:T(8,128)(2,1)S(1)}, bf16[4,128,768]{2,1,0:T(8,128)(2,1)S(1)}, u32[]{:S(2)}, u32[]{:S(2)}) collective-permute-start(bf16[4,128,768]{2,1,0:T(8,128)(2,1)S(1)} %get-tuple-element.286), channel_id=1, source_target_pairs={{0,1},{1,0},{2,3},{3,2},{4,5},{5,4},{6,7},{7,6},{8,9},{9,8},{10,11... | collective-permute-start | bytes 2359304 | tf_op jit(solution)/shard_map/ppermute | solution.py:18
  758.4 70.1 %collective-permute-start.7 = (bf16[4,256,768]{2,1,0:T(8,128)(2,1)}, bf16[4,256,768]{2,1,0:T(8,128)(2,1)}, u32[]{:S(2)}, u32[]{:S(2)}) collective-permute-start(bf16[4,256,768]{2,1,0:T(8,128)(2,1)} %maximum_select_fusion.7), channel_id=1, source_target_pairs={{0,2},{1,3},{2,0},{3,1},{4,6},{5,7},{6,4},{7,5},{8,10},{9,11},{10,... | collective-permute-start | bytes 4718600 | tf_op jit(solution)/shard_map/ppermute | solution.py:18
  761.2 72.6 %copy-start.8 = (f32[12,512,64]{1,2,0:T(8,128)S(1)}, f32[12,512,64]{1,2,0:T(8,128)}, u32[]{:S(2)}) copy-start(f32[12,512,64]{1,2,0:T(8,128)} %copy-done.7) | copy-start | bytes 4718596
  989.9 78.3 %reduce-scatter.15.cloned.1.call-start = ((), (), s32[]{:S(2)}) async-start(), calls=%async_computation.16 | async-start | bytes 3932160 | tf_op jit(solution)/shard_map/reduce_scatter | solution.py:302
  990.7 215.2 %reduce-scatter.17.cloned.1.call-start = ((), (), s32[]{:S(2)}) async-start(), calls=%async_computation.17 | async-start | bytes 3932160 | tf_op jit(solution)/shard_map/reduce_scatter | solution.py:56
  994.7 73.5 %copy-start.23 = (bf16[768,192]{1,0:T(8,128)(2,1)S(1)}, bf16[768,192]{1,0:T(8,128)(2,1)}, u32[]{:S(2)}) copy-start(bf16[768,192]{1,0:T(8,128)(2,1)} %copy-done.22) | copy-start | bytes 884740
  1093.4 24.7 %all-to-all-start.1 = ((bf16[8,960,96]{1,2,0:T(8,128)(2,1)}), bf16[8,960,96]{1,2,0:T(8,128)(2,1)}, u32[]{:S(2)}, u32[]{:S(2)}) async-start(bf16[8,960,96]{1,2,0:T(8,128)(2,1)} %bitcast.236), calls=%async_computation.7 | async-start | bytes 3145728 | tf_op jit(solution)/shard_map/all_to_all | solution.py:34
  1118.1 84.3 %all-to-all-start = ((bf16[8,96,1344]{2,1,0:T(8,128)(2,1)}), bf16[8,96,1344]{2,1,0:T(8,128)(2,1)}, u32[]{:S(2)}, u32[]{:S(2)}) async-start(bf16[8,96,1344]{2,1,0:T(8,128)(2,1)} %bitcast.231), calls=%async_computation.6 | async-start | bytes 4325376 | tf_op jit(solution)/shard_map/all_to_all | solution.py:34
  1122.4 66.0 %copy-start.47 = (f32[768]{0:T(1024)S(1)}, f32[768]{0:T(1024)}, u32[]{:S(2)}) copy-start(f32[768]{0:T(1024)} %get-tuple-element.316) | copy-start | bytes 9220
  (55 other events, 810.6 us)
Sparse Core Ops, SparseCore 0:
  105.3 31.0 all-gather.6
  138.6 28.4 all-gather.4
  313.1 60.3 reduce-scatter.6
  500.2 60.3 reduce-scatter.8
  670.6 60.4 reduce-scatter.10
  990.1 37.8 reduce-scatter.12
  1030.5 37.7 reduce-scatter.14
  1076.0 60.4 reduce-scatter.16
Sparse Core Ops, SparseCore 1:
  377.8 24.3 all-gather.8
  403.9 23.8 all-gather.10
